TPU v7x, 32 devices: a whole 2x2x4 slice. The times are simulated.
32 devices in a mesh: row: 16 (over z, y, x), col: 2 (over core).
Axes of the slice: x: 2, y: 2, z: 4, core: 2. Of those that a mesh axis runs over, the one named last changes fastest.
Arguments:
- image_embeddings: bfloat16 [128, 64, 1024], P('row', 'col'), may hold values from -6 to 6
- lagged_blend_ratios: float32 [3, 1024], replicated, may hold values from 0.05 to 0.95
- linear_map_coefficients: bfloat16 [3, 1024, 1024], P(None, 'row'), may hold values from -0.1875 to 0.1875
- retention_exponent: float32 [16, 128, 64], P(None, 'row', 'col'), may hold values from -3 to 0, as said below
- self_credit: float32 [1024], replicated, may hold values from 1 to 8
- channel_scale_vector: float32 [1024], replicated, may hold values from 0.5 to 2
- pooling_scale_vector: float32 [4096], replicated, may hold values from 0.5 to 2
- pooling_offset_vector: float32 [4096], replicated, may hold values from -3 to 3
Outputs:
- merged: bfloat16 [64, 32, 4096], P('row', 'col')
Inputs may be any that keep to these rules, and one draw needn't show every extreme that they name: `retention_exponent`: the logarithm of the share of a head's state kept at each patch.
All inputs are finite; a program needn't handle non-finite values.
Results may differ from a plain program's by a relative error of at most 0.0057.
Values may be sent and summed in bfloat16 or wider, within the bound.
A program may use at most 192 MiB of HBM per device.

v0:
```python
import jax
import jax.numpy as jnp
from jax import lax
from jax.sharding import PartitionSpec as P

PRECISE = lax.Precision.HIGHEST


def extended(cells, sides, width):
    for axis, dim in sides:
        count = lax.axis_size(axis)
        ends = count - 1
        head = lax.slice_in_dim(cells, 0, width, axis=dim)
        tail = lax.slice_in_dim(cells, cells.shape[dim] - width, cells.shape[dim], axis=dim)
        cells = jnp.concatenate(
            [
                lax.ppermute(tail, axis, [(i, (i + 1) % count) for i in range(ends)]),
                cells,
                lax.ppermute(head, axis, [((i + 1) % count, i) for i in range(ends)]),
            ],
            axis=dim,
        )
    return cells


def entering(array, axis, combine, identity, reverse):
    size, position = (lax.axis_size(axis), lax.axis_index(axis))
    everything = jax.tree.map(lambda part: lax.all_gather(part, axis), array)
    start = jax.tree.map(
        lambda part, zero: jnp.broadcast_to(jnp.asarray(zero, part.dtype), part.shape),
        array,
        identity,
    )

    def hop(k, before):
        at = size - 1 - k if reverse else k
        reached = at > position if reverse else at < position
        new = combine(before, jax.tree.map(lambda part: part[at], everything))
        return jax.tree.map(lambda a, b: jnp.where(reached, a, b), new, before)

    return lax.fori_loop(0, size, hop, start)


def head_mix(argument_tensors):
    query_head, key_head, value_head, running, before = argument_tensors
    count = query_head.shape[0]
    position = jnp.arange(count, dtype=jnp.int32)
    earlier_mask = position[:, None] > position[None, :]
    diagonal = position[:, None] == position[None, :]
    scores = jnp.einsum("td,sd->ts", query_head, key_head, preferred_element_type=jnp.float32)
    exponent = jnp.where(
        earlier_mask, before[:, None] - running[None, :], before[None, :] - running[:, None]
    )
    weights = jnp.where(diagonal, jnp.float32(0.0), jnp.exp(exponent))
    pair_weight = (scores * weights).astype(jnp.bfloat16)
    return jnp.dot(pair_weight, value_head, preferred_element_type=jnp.float32)


def chain_states(earlier, later_part):
    return (earlier[0] * later_part[0], later_part[0][..., None, None] * earlier[1] + later_part[1])


def body(
    image_embeddings,
    lagged_blend_ratios,
    linear_map_coefficients,
    retention_exponent,
    self_credit,
    channel_scale_vector,
    pooling_scale_vector,
    pooling_offset_vector,
):
    tile_rows, tile_cols, width = image_embeddings.shape
    quarter = width // 4
    attention_units = retention_exponent.shape[0]
    unit_dimension = width // attention_units
    count = tile_rows * tile_cols
    col_edges = jnp.concatenate(
        [image_embeddings[:, :1, quarter : 2 * quarter], image_embeddings[:, -1:, :quarter]], axis=1
    )
    col_padded = extended(col_edges, (("col", 1),), 1)
    row_edges = jnp.concatenate(
        [
            image_embeddings[:1, :, 3 * quarter :],
            image_embeddings[-1:, :, 2 * quarter : 3 * quarter],
        ],
        axis=0,
    )
    row_padded = extended(row_edges, (("row", 0),), 1)
    shifted = jnp.concatenate(
        [
            jnp.concatenate([col_padded[:, :1], image_embeddings[:, :-1, :quarter]], axis=1),
            jnp.concatenate(
                [image_embeddings[:, 1:, quarter : 2 * quarter], col_padded[:, 3:]], axis=1
            ),
            jnp.concatenate(
                [row_padded[:1], image_embeddings[:-1, :, 2 * quarter : 3 * quarter]], axis=0
            ),
            jnp.concatenate([image_embeddings[1:, :, 3 * quarter :], row_padded[3:]], axis=0),
        ],
        axis=2,
    )
    content_vectors_full = image_embeddings.astype(jnp.float32)
    shifted_float = shifted.astype(jnp.float32)
    coeffs = lagged_blend_ratios[:, None, None, :]
    mixed = (content_vectors_full[None] * coeffs + shifted_float[None] * (1.0 - coeffs)).astype(
        jnp.bfloat16
    )
    mixed = mixed.reshape(3, count, width)
    gathered = lax.all_gather(linear_map_coefficients, "row", axis=1, tiled=True)
    mapped_embeddings = jnp.einsum(
        "ptd,pde->pte", mixed, gathered, preferred_element_type=jnp.float32
    )
    mapped_embeddings = mapped_embeddings.astype(jnp.bfloat16)
    acceptance_vectors, address_vectors, content_vectors = (
        mapped_embeddings[0],
        mapped_embeddings[1],
        mapped_embeddings[2],
    )
    retention_ratio = retention_exponent.reshape(attention_units, count)
    running = jnp.cumsum(retention_ratio, axis=1)
    before = running - retention_ratio
    total = running[:, -1:]
    unitwise_probes = acceptance_vectors.astype(jnp.float32).reshape(
        count, attention_units, unit_dimension
    )
    unitwise_addresses = address_vectors.astype(jnp.float32).reshape(
        count, attention_units, unit_dimension
    )
    unitwise_contents = content_vectors.astype(jnp.float32).reshape(
        count, attention_units, unit_dimension
    )
    forward_summary = jnp.einsum(
        "thd,the->hde",
        unitwise_addresses * jnp.exp(total - running).T[:, :, None],
        unitwise_contents,
        precision=PRECISE,
    )
    backward_summary = jnp.einsum(
        "thd,the->hde",
        unitwise_addresses * jnp.exp(before).T[:, :, None],
        unitwise_contents,
        precision=PRECISE,
    )
    kept = jnp.exp(total[:, 0])
    identity = (jnp.ones_like(kept), jnp.zeros_like(forward_summary))
    ordered_sequence = entering((kept, forward_summary), "row", chain_states, identity, False)[1]
    reversed_sequence = entering((kept, backward_summary), "row", chain_states, identity, True)[1]

    def per_head(matrix):
        return matrix.reshape(count, attention_units, unit_dimension).transpose(1, 0, 2)

    local = lax.map(
        head_mix,
        (
            per_head(acceptance_vectors),
            per_head(address_vectors),
            per_head(content_vectors),
            running,
            before,
        ),
    )
    carried = jnp.exp(before).T[:, :, None] * jnp.einsum(
        "thd,hde->the", unitwise_probes, ordered_sequence, precision=PRECISE
    )
    carried = carried + jnp.exp(total - running).T[:, :, None] * jnp.einsum(
        "thd,hde->the", unitwise_probes, reversed_sequence, precision=PRECISE
    )
    principal_summand = (
        jnp.sum(
            unitwise_probes
            * self_credit.reshape(attention_units, unit_dimension)
            * unitwise_addresses,
            axis=2,
            keepdims=True,
        )
        * unitwise_contents
    )
    wkv_out = local.transpose(1, 0, 2) + carried + principal_summand
    centred = wkv_out - jnp.mean(wkv_out, axis=2, keepdims=True)
    variance = jnp.mean(centred * centred, axis=2, keepdims=True)
    normed = (
        centred
        * lax.rsqrt(variance + 1e-05)
        * channel_scale_vector.reshape(attention_units, unit_dimension)
    )
    block_out = content_vectors_full.reshape(count, attention_units, unit_dimension) + normed
    grouped = block_out.reshape(tile_rows // 2, 2, tile_cols // 2, 2, width).transpose(
        0, 2, 3, 1, 4
    )
    grouped = grouped.reshape(tile_rows // 2, tile_cols // 2, 4 * width)
    merge_centred = grouped - jnp.mean(grouped, axis=2, keepdims=True)
    merge_variance = jnp.mean(merge_centred * merge_centred, axis=2, keepdims=True)
    return (
        merge_centred * lax.rsqrt(merge_variance + 1e-05) * pooling_scale_vector
        + pooling_offset_vector
    ).astype(jnp.bfloat16)


def solution(mesh):
    return jax.shard_map(
        body,
        mesh=mesh,
        in_specs=(
            P("row", "col", None),
            P(),
            P(None, "row", None),
            P(None, "row", "col"),
            P(),
            P(),
            P(),
            P(),
        ),
        out_specs=P("row", "col", None),
        check_vma=False,
    )
```

profile of v0, /device:TPU:0, one launch (start us, length us, event | category | flops | bytes accessed | tf_op | source)
XLA Modules:
  0.0 375.1 jit_solution(2178739914577812114)
XLA Ops:
  8.1 2.4 collective-permute-start
  10.5 1.3 collective-permute-start.1
  12.5 4.2 %collective-permute-start.2 = (bf16[1,32,256]{2,1,0:T(8,128)(2,1)S(1)}, bf16[1,32,256]{2,1,0:T(8,128)(2,1)S(1)}, u32[]{:S(2)}, u32[]{:S(2)}) collective-permute-start(bf16[1,32,256]{2,1,0:T(8,128)(2,1)S(1)} %get-tuple-element.375), channel_id=1, source_target_pairs={{0,2},{2,4},{4,6},{6,8},{8,10},{10,12},{12,14},{14,16},{16,18},{18... | collective-permute-start | bytes 49160 | tf_op jit(solution)/shard_map/ppermute | solution.py:17
  16.8 1.3 collective-permute-start.3
  25.3 81.0 %all-gather.7.cloned.1.call-done = bf16[3,1024,1024]{2,1,0:T(8,128)(2,1)} async-done(((bf16[3,64,1024]{2,1,0:T(8,128)(2,1)}), bf16[3,1024,1024]{2,1,0:T(8,128)(2,1)}) %all-gather.7.cloned.1.call-update) | async-done | bytes 6291472 | tf_op jit(solution)/shard_map/all_gather | solution.py:110
  106.3 4.6 %convolution_convert_fusion = bf16[3,256,1024]{2,1,0:T(8,128)(2,1)S(1)} fusion(bf16[3,1024,1024]{2,1,0:T(8,128)(2,1)} %all-gather.7.cloned.1.call-done, f32[3,1024]{1,0:T(4,128)S(1)} %broadcast_subtract_fusion, f32[256,1024]{1,0:T(8,128)S(1)} %maximum_convert_fusion, f32[3,1024]{1,0:T(4,128)S(1)} %copy-done.4, f32[256,1024]{1,0:T(8,128)S(1)} %bitcast.121), kind=kOutput, calls=%fused_computation.35 | convolution fusion | flops 1614544896 | bytes 9986048 | tf_op jit(solution)/shard_map/ptd,pde->pte/dot_general | solution.py:111
  111.5 1.4 fusion.41
  113.1 2.0 reshape.121
  116.6 40.7 %all-reduce = f32[256]{0:T(256)S(1)} all-reduce(f32[256]{0:T(256)S(1)} %dynamic-update-slice), channel_id=2, replica_groups=mesh['row'=16,'col'=2] {'row'}, use_global_device_ids=true, to_apply=%add | all-reduce | flops 256 | bytes 2048
  157.4 3.5 copy.59
  161.1 1.4 fusion.40
  162.6 16.1 %while.40 = (s32[]{:T(128)}, f32[16,256,64]{1,2,0:T(8,128)}, bf16[16,256,64]{1,2,0:T(8,128)(2,1)S(1)}, bf16[16,256,64]{1,2,0:T(8,128)(2,1)S(1)}, f32[16,256]{1,0...) while((s32[]{:T(128)}, f32[16,256,64]{1,2,0:T(8,128)}, ...), condition=%wide.region_3.4_spmd, body=%wide.region_2.3_spmd.sunk | while | flops 17301504 | bytes 174177 | solution.py:153
  178.7 45.9 %all-gather.11.cloned.1.call-done = f32[256,64,64]{2,1,0:T(8,128)} async-done(((f32[16,64,64]{2,1,0:T(8,128)}), f32[256,64,64]{2,1,0:T(8,128)}) %all-gather.11.cloned.1.call-update) | async-done | bytes 4194320 | tf_op jit(solution)/shard_map/all_gather | solution.py:28
  224.6 19.6 %while.42 = (s32[]{:T(128)}, f32[16,64,64]{2,1,0:T(8,128)S(1)}, s32[]{:T(128)}, f32[16,16]{1,0:T(8,128)S(1)}, f32[16,16,64,64]{3,2,1,0:T(8,128)}, /*index=5*/s32[]{:T(128)}, s32[]{:T(128)}, s32[]{:T(128)}, s32[]{:T(128)}) while((s32[]{:T(128)}, f32[16,64,64]{2,1,0:T(8,128)S(1)}, s32[]{:T(128)}, f32[16,16]{1,0:T(8,128)S(1)}, ...), condition=%wide.region_7.8_spmd.clone, body=%wide.region_6.7_spmd.clone.sunk | while | flops 262152 | bytes 786799 | solution.py:41
  227.1 1.2 fusion.72
  230.7 1.2 fusion.72
  233.2 1.2 fusion.72
  234.5 1.2 fusion.72
  236.9 1.2 fusion.72
  239.4 1.2 fusion.72
  240.6 1.2 fusion.72
  241.8 1.2 fusion.72
  243.1 1.2 fusion.72
  244.3 93.6 %all-gather.9.cloned.1.call-done = f32[256,64,64]{2,1,0:T(8,128)} async-done(((f32[16,64,64]{2,1,0:T(8,128)}), f32[256,64,64]{2,1,0:T(8,128)}) %all-gather.9.cloned.1.call-update) | async-done | bytes 4194320 | tf_op jit(solution)/shard_map/all_gather | solution.py:28
  337.9 19.4 %while.41 = (s32[]{:T(128)}, f32[16,64,64]{2,1,0:T(8,128)S(1)}, s32[]{:T(128)}, f32[16,16]{1,0:T(8,128)S(1)}, f32[16,16,64,64]{3,2,1,0:T(8,128)}, /*index=5*/s32[]{:T(128)}, s32[]{:T(128)}) while((s32[]{:T(128)}, f32[16,64,64]{2,1,0:T(8,128)S(1)}, s32[]{:T(128)}, f32[16,16]{1,0:T(8,128)S(1)}, f32[16,16,64,64]{3,2,1,0:T(8,128)}, ...), condition=%wide.region_5.6_spmd.clone, body=%wide.region_4.5_spmd.clone.sunk | while | flops 262148 | bytes 786737 | solution.py:41
  340.3 1.2 fusion.71
  341.5 1.2 fusion.71
  345.2 1.2 fusion.71
  346.4 1.2 fusion.71
  358.0 1.9 fusion.38
  359.9 1.9 fusion.53
  362.3 1.3 copy.60
  (156 shorter events, 56.0 us)
Async XLA Ops:
  6.5 99.8 %copy-start.4 = (f32[3,1024]{1,0:T(4,128)S(1)}, f32[3,1024]{1,0:T(4,128)}, u32[]{:S(2)}) copy-start(f32[3,1024]{1,0:T(4,128)} %param.15) | copy-start | bytes 36868
  6.5 99.8 %all-gather.7.cloned.1.call-start = ((), (), s32[]{:S(2)}) async-start(), calls=%async_computation | async-start | bytes 6684672 | tf_op jit(solution)/shard_map/all_gather | solution.py:110
  7.3 217.4 %all-gather.11.cloned.1.call-start = ((), (), s32[]{:S(2)}) async-start(), calls=%async_computation.2 | async-start | bytes 8912896 | tf_op jit(solution)/shard_map/all_gather | solution.py:28
  8.1 16.9 %collective-permute-start = (bf16[8,1,256]{2,1,0:T(2,128)(2,1)S(1)}, bf16[8,1,256]{2,1,0:T(2,128)(2,1)S(1)}, u32[]{:S(2)}, u32[]{:S(2)}) collective-permute-start(bf16[8,1,256]{2,1,0:T(2,128)(2,1)S(1)} %get-tuple-element.371), channel_id=1, source_target_pairs={{0,1},{2,3},{4,5},{6,7},{8,9},{10,11},{12,13},{14,15},{16,17},{18,... | collective-permute-start | bytes 12296 | tf_op jit(solution)/shard_map/ppermute | solution.py:17
  10.5 14.5 %collective-permute-start.1 = (bf16[8,1,256]{2,1,0:T(2,128)(2,1)S(1)}, bf16[8,1,256]{2,1,0:T(2,128)(2,1)S(1)}, u32[]{:S(2)}, u32[]{:S(2)}) collective-permute-start(bf16[8,1,256]{2,1,0:T(2,128)(2,1)S(1)} %get-tuple-element.372), channel_id=1, source_target_pairs={{1,0},{3,2},{5,4},{7,6},{9,8},{11,10},{13,12},{15,14},{17,16},{19,... | collective-permute-start | bytes 12296 | tf_op jit(solution)/shard_map/ppermute | solution.py:19
  12.5 12.5 %collective-permute-start.2 = (bf16[1,32,256]{2,1,0:T(8,128)(2,1)S(1)}, bf16[1,32,256]{2,1,0:T(8,128)(2,1)S(1)}, u32[]{:S(2)}, u32[]{:S(2)}) collective-permute-start(bf16[1,32,256]{2,1,0:T(8,128)(2,1)S(1)} %get-tuple-element.375), channel_id=1, source_target_pairs={{0,2},{2,4},{4,6},{6,8},{8,10},{10,12},{12,14},{14,16},{16,18},{18... | collective-permute-start | bytes 49160 | tf_op jit(solution)/shard_map/ppermute | solution.py:17
  16.8 8.4 %collective-permute-start.3 = (bf16[1,32,256]{2,1,0:T(8,128)(2,1)S(1)}, bf16[1,32,256]{2,1,0:T(8,128)(2,1)S(1)}, u32[]{:S(2)}, u32[]{:S(2)}) collective-permute-start(bf16[1,32,256]{2,1,0:T(8,128)(2,1)S(1)} %get-tuple-element.376), channel_id=1, source_target_pairs={{2,0},{4,2},{6,4},{8,6},{10,8},{12,10},{14,12},{16,14},{18,16},{20... | collective-permute-start | bytes 49160 | tf_op jit(solution)/shard_map/ppermute | solution.py:19
  110.9 2.2 copy-start
  111.3 3.8 %copy-start.5 = (f32[1024]{0:T(1024)S(1)}, f32[1024]{0:T(1024)}, u32[]{:S(2)}) copy-start(f32[1024]{0:T(1024)} %param.18) | copy-start | bytes 12292
  111.3 3.8 %copy-start.6 = (f32[1024]{0:T(1024)S(1)}, f32[1024]{0:T(1024)}, u32[]{:S(2)}) copy-start(f32[1024]{0:T(1024)} %param.19) | copy-start | bytes 12292
  111.3 3.9 %copy-start.7 = (u32[32]{0:T(128)S(1)}, u32[32]{0:T(128)}, u32[]{:S(2)}) copy-start(u32[32]{0:T(128)} %constant.112) | copy-start | bytes 388
  113.0 224.9 %all-gather.9.cloned.1.call-start = ((), (), s32[]{:S(2)}) async-start(), calls=%async_computation.1 | async-start | bytes 8912896 | tf_op jit(solution)/shard_map/all_gather | solution.py:28
  359.9 2.1 copy-start.1
  364.6 2.9 copy-start.2
  364.6 2.9 copy-start.3
Sparse Core Ops, SparseCore 0:
  10.1 96.1 all-gather.6
  113.1 111.4 all-gather.10
  227.4 110.4 all-gather.8
where the time goes:
time: 377 us; the launch traced here: 375 us
  waiting for transfers between devices  221 us (59%)
  other arithmetic  45 us (12%)
  blocking collectives  40.7 us (11%)
  matrix products  25.9 us (7%)
  local copies, waits for them, and re-layouts  17.6 us (5%)
  between operations  14.1 us (4%)
  starting transfers between devices  9.26 us (2%)
    all_gather x2, waiting for transfers between devices, entering(): everything = jax.tree.map(lambda part: lax.all_gather(part, axis), array)  140 us
    all_gather x1, waiting for transfers between devices, body(): lax.all_gather(linear_map_coefficients, 'row', axis=1, tiled=True)  81 us
    unnamed x1, blocking collectives  40.7 us
    select_n x32, other arithmetic, hop(): return jax.tree.map(lambda a, b: jnp.where(reached, a, b), new, before)  37.7 us
    dot_general x16, matrix products, head_mix(): return jnp.dot(pair_weight, value_head, preferred_element_type=jnp.float32)  15.9 us
  transfers between devices with their start and end apart: 7, of which 3 were waited for; matrix products, arithmetic and copies ran while one was open for 14% of the time, Pallas kernels for 0%

commit v1 on v0

v1 whole, which is shorter than its diff:
```python
import functools

import jax
import jax.numpy as jnp
from jax import lax
from jax.experimental import pallas as pl
from jax.experimental.pallas import tpu as pltpu
from jax.sharding import PartitionSpec as P

MESH = pl.DeviceIdType.MESH
F32 = jnp.float32
BF16 = jnp.bfloat16
HIGH = lax.Precision.HIGHEST
UP, DOWN, FIRST, SECOND, MATE = range(5)


def iota(shape, dim):
    return lax.broadcasted_iota(jnp.int32, shape, dim)


def kernel(
    rows, cols, tile_rows, tile_cols, heads,
    x_ref, ratio_ref, w_ref, ret_ref, credit_ref, gain_ref, scale_ref, offset_ref,
    out_ref,
    wf, mx, proj, decay, halo_side, halo_row, run_c, mine, totals, states, arrived, scan_f, leaving,
    entering, block, stats,
    w_send, w_recv, halo_send, halo_recv, t_send, t_recv, a_send, a_recv, b_send, b_recv,
):
    count, width = x_ref.shape
    hd = width // heads
    pairs = heads // 2
    lanes = 2 * hd
    quarter = width // 4
    share = w_ref.shape[1]
    half_w = width // 2
    unit = states.shape[1]
    row, col = lax.axis_index("row"), lax.axis_index("col")
    plane = 4
    depth = rows // plane
    z, q = row // plane, row % plane
    bx, by = q % 2, q // 2
    half = col % 2
    mate = col + 1 - 2 * half
    q1 = (1 - half) * (q + 1 - 2 * bx) + half * (q + 2 - 4 * by)
    q2 = half * (q + 1 - 2 * bx) + (1 - half) * (q + 2 - 4 * by)
    q12 = plane - 1 - q

    barrier = pltpu.get_barrier_semaphore()

    def greet(o, carry):
        pl.semaphore_signal(barrier, inc=1, device_id={"row": (row + o) % rows}, device_id_type=MESH)
        return carry

    lax.fori_loop(1, rows, greet, 0)
    right, left = (col + 1) % cols, (col + cols - 1) % cols
    for other in (right, left, mate):
        pl.semaphore_signal(barrier, inc=1, device_id={"col": other}, device_id_type=MESH)
    pl.semaphore_wait(barrier, rows + 2)

    down_row, up_row = (row + 1) % rows, (row + rows - 1) % rows
    halos = [
        pltpu.make_async_remote_copy(
            x_ref.at[:, 0:quarter], halo_side.at[0], halo_send.at[0], halo_recv.at[0],
            device_id={"col": right}, device_id_type=MESH),
        pltpu.make_async_remote_copy(
            x_ref.at[:, quarter:2 * quarter], halo_side.at[1], halo_send.at[1], halo_recv.at[1],
            device_id={"col": left}, device_id_type=MESH),
        pltpu.make_async_remote_copy(
            x_ref.at[count - tile_cols:count, 2 * quarter:3 * quarter], halo_row.at[0],
            halo_send.at[2], halo_recv.at[2], device_id={"row": down_row}, device_id_type=MESH),
        pltpu.make_async_remote_copy(
            x_ref.at[0:tile_cols, 3 * quarter:], halo_row.at[1],
            halo_send.at[3], halo_recv.at[3], device_id={"row": up_row}, device_id_type=MESH),
    ]
    for h in halos:
        h.start()

    def sl(g):
        return pl.ds(1, 2) if g == 0 else pl.ds(0, 1)

    def place(g, side, src):
        return wf.at[sl(g), side, pl.ds(pl.multiple_of(src * share, share), share), :]

    targets = {
        UP: {"row": (row + plane) % rows},
        DOWN: {"row": (row + rows - plane) % rows},
        FIRST: {"row": z * plane + q1},
        SECOND: {"row": z * plane + q2},
        MATE: {"col": mate},
    }

    def send(g, kind, src, own=False):
        source = place(g, half, src)
        if own:
            source = w_ref.at[sl(g), :, pl.ds(pl.multiple_of(half * half_w, half_w), half_w)]
        return pltpu.make_async_remote_copy(
            source, place(g, half, src), w_send.at[g, kind, src], w_recv.at[g, half, src],
            device_id=targets[kind], device_id_type=MESH)

    def got(g, side, src):
        ref = place(g, side, src)
        pltpu.make_async_remote_copy(
            ref, ref, w_send.at[g, MATE, src], w_recv.at[g, side, src],
            device_id=targets[MATE], device_id_type=MESH).wait_recv()

    can_up, can_down = z < depth - 1, z > 0

    def own_step(g):
        @pl.when(can_up)
        def _():
            send(g, UP, row, True).start()

        @pl.when(can_down)
        def _():
            send(g, DOWN, row, True).start()

        send(g, SECOND, row, True).start()
        send(g, FIRST, row, True).start()

    def both(d, act):
        if d == 0:
            act(z, None)
            return

        @pl.when(z >= d)
        def _():
            act(z - d, UP)

        @pl.when(z + d < depth)
        def _():
            act(z + d, DOWN)

    def z_step(g, d):
        def act(zz, onward):
            src = zz * plane + q
            got(g, half, src)

            @pl.when(can_up if onward == UP else can_down)
            def _():
                send(g, onward, src).start()

            for kind in (SECOND, FIRST, MATE):
                send(g, kind, src).start()

        both(d, act)

    def first_step(g, d):
        def act(zz, onward):
            src = zz * plane + q1
            got(g, half, src)
            send(g, SECOND, src).start()
            send(g, MATE, src).start()

        both(d, act)

    def second_step(g, d):
        def act(zz, onward):
            for qq in (q2, q12):
                src = zz * plane + qq
                got(g, half, src)
                send(g, MATE, src).start()

        both(d, act)

    def mate_wait(g):
        def one(o, carry):
            got(g, 1 - half, (row + o) % rows)
            return carry

        lax.fori_loop(1, rows, one, 0)

    own_step(0)

    at = pl.ds(pl.multiple_of(row * share, share), share)
    for p in range(3):
        for side in range(2):
            wf[p, side, at, :] = w_ref[p, :, side * half_w:(side + 1) * half_w]

    ret = ret_ref[...]
    tri = (iota((count, count), 0) >= iota((count, count), 1)).astype(F32)
    running_c = lax.dot_general(tri, ret, (((1,), (1,)), ((), ())), precision=HIGH, preferred_element_type=F32)
    running_r = lax.dot_general(ret, tri, (((1,), (1,)), ((), ())), precision=HIGH, preferred_element_type=F32)
    eye = (iota((count, count), 0) == iota((count, count), 1)).astype(F32)
    ret_c = lax.dot_general(eye, ret, (((1,), (1,)), ((), ())), precision=HIGH, preferred_element_type=F32)
    before_c = running_c - ret_c
    before_r = running_r - ret
    total_r = running_c[count - 1:count, :]
    run_c[0] = running_c
    run_c[1] = before_c
    run_c[2] = total_r - running_c
    mine[...] = jnp.broadcast_to(
        jnp.concatenate([total_r, jnp.zeros((1, 128 - heads), F32)], axis=1), (8, 128))
    totals[row] = mine[...]

    def picked(table, h):
        return jnp.sum(jnp.where(iota(table.shape, 1) == h, table, 0.0), axis=1, keepdims=True)

    def picked_row(table, h):
        return jnp.sum(jnp.where(iota(table.shape, 0) == h, table, 0.0), axis=0, keepdims=True)

    def total_copy(o):
        to = (row + o) % rows
        return pltpu.make_async_remote_copy(
            mine, totals.at[row], t_send.at[to], t_recv.at[row],
            device_id={"row": to}, device_id_type=MESH)

    def total_send(o, carry):
        total_copy(o).start()
        return carry

    lax.fori_loop(1, rows, total_send, 0)

    z_step(0, 1) if depth > 1 else None
    first_step(0, 0)
    second_step(0, 0)

    for h in halos:
        h.wait()
    token = iota((count, quarter), 0)
    place_in_row = token % tile_cols
    x0 = x_ref[:, 0:quarter].astype(F32)
    x1 = x_ref[:, quarter:2 * quarter].astype(F32)
    side0 = jnp.where(col > 0, halo_side[0].astype(F32), 0.0)
    side1 = jnp.where(col < cols - 1, halo_side[1].astype(F32), 0.0)
    top = jnp.where(row > 0, halo_row[0].astype(F32), 0.0)
    bottom = jnp.where(row < rows - 1, halo_row[1].astype(F32), 0.0)
    last = tile_cols - 1
    shifted = [
        jnp.where(place_in_row == 0, pltpu.roll(side0, count - last, 0), pltpu.roll(x0, 1, 0)),
        jnp.where(place_in_row == last, pltpu.roll(side1, last, 0), pltpu.roll(x1, count - 1, 0)),
        jnp.concatenate([top, x_ref[0:count - tile_cols, 2 * quarter:3 * quarter].astype(F32)], axis=0),
        jnp.concatenate([x_ref[tile_cols:count, 3 * quarter:].astype(F32), bottom], axis=0),
    ]
    for part in range(4):
        span = slice(part * quarter, (part + 1) * quarter)
        xs = x_ref[:, span].astype(F32)
        for p in range(3):
            c = ratio_ref[p:p + 1, span]
            mx[p, :, span] = (xs * c + shifted[part] * (1.0 - c)).astype(BF16)

    for d in range(2, depth):
        z_step(0, d)
        first_step(0, d - 1)
        second_step(0, d - 1)
    if depth > 1:
        first_step(0, depth - 1)
        second_step(0, depth - 1)
    own_step(1)

    earlier = iota((count, count), 0) > iota((count, count), 1)
    diagonal = iota((count, count), 0) == iota((count, count), 1)

    def decays(h, carry):
        rc, bc = picked(run_c[0], h), picked(run_c[1], h)
        rr, br = picked_row(running_r, h), picked_row(before_r, h)
        exponent = jnp.where(earlier, bc - rr, br - rc)
        decay[h] = jnp.where(diagonal, 0.0, jnp.exp(exponent))
        return carry

    lax.fori_loop(0, heads, decays, 0)

    mate_wait(0)

    def project(p):
        for side in range(2):
            def chunk(i, carry):
                src = pl.ds(pl.multiple_of(i * 256, 256), 256)
                dst = pl.ds(pl.multiple_of(side * half_w + i * 256, 256), 256)
                proj[p, :, dst] = jnp.dot(
                    mx[p], wf[p, side, :, src], preferred_element_type=F32).astype(BF16)
                return carry

            lax.fori_loop(0, half_w // 256, chunk, 0)

    project(1)
    project(2)

    lane = iota((count, lanes), 1)
    low = lane < hd

    def pair_col(table, i):
        return jnp.where(low, picked(table, 2 * i), picked(table, 2 * i + 1))

    low_u = iota((hd, lanes), 1) < hd
    flat = rows * unit

    def local_states(i, carry):
        span = pl.ds(pl.multiple_of(i * lanes, lanes), lanes)
        k = proj[1, :, span].astype(F32)
        v = proj[2, :, span]
        kd = jnp.concatenate(
            [k * jnp.exp(pair_col(run_c[2], i)), k * jnp.exp(pair_col(run_c[1], i))], axis=1).astype(BF16)
        m = lax.dot_general(kd, v, (((0,), (0,)), ((), ())), preferred_element_type=F32)
        a = jnp.where(low_u, m[0:hd], pltpu.roll(m[2 * hd:3 * hd], hd, 1)).astype(BF16)
        b = jnp.where(low_u, pltpu.roll(m[hd:2 * hd], hd, 1), m[3 * hd:]).astype(BF16)
        per = hd // unit
        for s in range(per):
            states[2 * i * per + s] = a[s * unit:(s + 1) * unit]
            states[(2 * i + 1) * per + s] = b[s * unit:(s + 1) * unit]
        return carry

    lax.fori_loop(0, pairs, local_states, 0)

    def a_copy(o):
        to = (row + o) % rows
        return pltpu.make_async_remote_copy(
            states.at[to], arrived.at[row], a_send.at[to], a_recv.at[row],
            device_id={"row": to}, device_id_type=MESH)

    def a_start(o, carry):
        a_copy(o).start()
        return carry

    lax.fori_loop(1, rows, a_start, 0)
    arrived[row] = states[row]

    z_step(1, 1) if depth > 1 else None
    first_step(1, 0)
    second_step(1, 0)
    if depth > 2:
        z_step(1, 2)
        first_step(1, 1)
        second_step(1, 1)

    def from_all(dst, send_sem, recv_sem):
        def one(o, carry):
            src = (row + o) % rows
            pltpu.make_async_remote_copy(
                dst.at[src], dst.at[src], send_sem.at[src], recv_sem.at[src],
                device_id={"row": src}, device_id_type=MESH).wait_recv()
            return carry

        lax.fori_loop(1, rows, one, 0)

    from_all(totals, t_send, t_recv)
    from_all(arrived, a_send, a_recv)
    head = (row * unit) // hd

    def kept(j):
        return jnp.exp(picked(totals[j], head))[0:1, :]

    def forward(j, acc):
        scan_f[j] = acc
        return kept(j) * acc + arrived[j].astype(F32)

    def backward(o, acc):
        j = rows - 1 - o
        leaving[j] = jnp.where(iota((unit, lanes), 1) < hd, scan_f[j], acc).astype(BF16)
        return kept(j) * acc + arrived[j].astype(F32)

    lax.fori_loop(0, rows, forward, jnp.zeros((unit, lanes), F32))
    lax.fori_loop(0, rows, backward, jnp.zeros((unit, lanes), F32))

    def b_copy(o):
        to = (row + o) % rows
        return pltpu.make_async_remote_copy(
            leaving.at[to], entering.at[row], b_send.at[to], b_recv.at[row],
            device_id={"row": to}, device_id_type=MESH)

    def b_start(o, carry):
        b_copy(o).start()
        return carry

    lax.fori_loop(1, rows, b_start, 0)
    entering[row] = leaving[row]

    for d in range(3, depth):
        z_step(1, d)
        first_step(1, d - 1)
        second_step(1, d - 1)
    if depth > 1:
        first_step(1, depth - 1)
        second_step(1, depth - 1)
    mate_wait(1)
    project(0)

    def halves(value):
        a = jnp.sum(jnp.where(low, value, 0.0), axis=1, keepdims=True)
        b = jnp.sum(jnp.where(low, 0.0, value), axis=1, keepdims=True)
        return jnp.where(low, a, b)

    def local_mix(i, carry):
        span = pl.ds(pl.multiple_of(i * lanes, lanes), lanes)
        r, k, v = proj[0, :, span], proj[1, :, span], proj[2, :, span]
        outs = []
        for s in range(2):
            rs = jnp.where(low if s == 0 else jnp.logical_not(low), r.astype(F32), 0.0).astype(BF16)
            scores = lax.dot_general(rs, k, (((1,), (1,)), ((), ())), preferred_element_type=F32)
            weight = (scores * decay[2 * i + s]).astype(BF16)
            outs.append(jnp.dot(weight, v, preferred_element_type=F32))
        own = halves(r.astype(F32) * credit_ref[:, span] * k.astype(F32)) * v.astype(F32)
        block[i] = jnp.where(low, outs[0], outs[1]) + own
        return carry

    lax.fori_loop(0, pairs, local_mix, 0)
    from_all(entering, b_send, b_recv)

    def finish(i, total):
        span = pl.ds(pl.multiple_of(i * lanes, lanes), lanes)
        r = proj[0, :, span]
        per = hd // unit
        a = jnp.concatenate([entering[2 * i * per + s].astype(F32) for s in range(per)], axis=0)
        b = jnp.concatenate([entering[(2 * i + 1) * per + s].astype(F32) for s in range(per)], axis=0)
        fwd = jnp.concatenate(
            [jnp.where(low_u, a, 0.0), jnp.where(low_u, 0.0, pltpu.roll(b, hd, 1))], axis=0).astype(BF16)
        bwd = jnp.concatenate(
            [jnp.where(low_u, pltpu.roll(a, hd, 1), 0.0), jnp.where(low_u, 0.0, b)], axis=0).astype(BF16)
        wkv = (
            block[i]
            + jnp.exp(pair_col(run_c[1], i)) * jnp.dot(r, fwd, preferred_element_type=F32)
            + jnp.exp(pair_col(run_c[2], i)) * jnp.dot(r, bwd, preferred_element_type=F32)
        )
        centred = wkv - halves(wkv) * (1.0 / hd)
        variance = halves(centred * centred) * (1.0 / hd)
        made = x_ref[:, span].astype(F32) + centred * lax.rsqrt(variance + 1e-05) * gain_ref[:, span]
        block[i] = made
        return total + made

    total = lax.fori_loop(0, pairs, finish, jnp.zeros((count, lanes), F32))
    group = (
        (iota((count, count), 0) // (2 * tile_cols) == iota((count, count), 1) // (2 * tile_cols))
        & (iota((count, count), 0) % tile_cols // 2 == iota((count, count), 1) % tile_cols // 2)
    ).astype(F32)

    def over_group(value):
        rowsum = jnp.broadcast_to(jnp.sum(value, axis=1, keepdims=True), (count, lanes))
        return jnp.dot(group, rowsum, precision=HIGH, preferred_element_type=F32) * (1.0 / (4 * width))

    mean = over_group(total)

    def spread(i, acc):
        dev = block[i] - mean
        return acc + dev * dev

    variance = over_group(lax.fori_loop(0, pairs, spread, jnp.zeros((count, lanes), F32)))
    stats[0] = mean
    stats[1] = lax.rsqrt(variance + 1e-05)
    half_cols = tile_cols // 2

    def emit(i, carry):
        for part in range(4):
            span = pl.ds(pl.multiple_of(part * width + i * lanes, lanes), lanes)
            g, o = scale_ref[:, span], offset_ref[:, span]
            for a in range(tile_rows // 2):
                take = pl.ds((2 * a + part % 2) * tile_cols + part // 2, half_cols, stride=2)
                value = (block[i, take, :] - stats[0, take, :]) * stats[1, take, :]
                out_ref[a, :, span] = (value * g + o).astype(BF16)
        return carry

    lax.fori_loop(0, pairs, emit, 0)

    def drain(o, carry):
        total_copy(o).wait_send()
        a_copy(o).wait_send()
        b_copy(o).wait_send()
        return carry

    lax.fori_loop(1, rows, drain, 0)
    for g in range(2):
        def z_drain(zz, carry):
            src = zz * plane + q

            @pl.when((zz <= z) & can_up)
            def _():
                send(g, UP, src).wait_send()

            @pl.when((zz >= z) & can_down)
            def _():
                send(g, DOWN, src).wait_send()

            send(g, FIRST, src).wait_send()
            send(g, SECOND, src).wait_send()
            send(g, SECOND, zz * plane + q1).wait_send()
            return carry

        lax.fori_loop(0, depth, z_drain, 0)

        def m_drain(o, carry):
            send(g, MATE, (row + o) % rows).wait_send()
            return carry

        lax.fori_loop(1, rows, m_drain, 0)


def body(x, ratios, w, retention, credit, gain, scale, offset):
    tile_rows, tile_cols, width = x.shape
    heads = retention.shape[0]
    count = tile_rows * tile_cols
    hd = width // heads
    rows, cols = lax.axis_size("row"), lax.axis_size("col")
    unit = heads * hd // rows
    pairs = heads // 2
    lanes = 2 * hd
    dma = pltpu.SemaphoreType.DMA
    return pl.pallas_call(
        functools.partial(kernel, rows, cols, tile_rows, tile_cols, heads),
        out_shape=jax.ShapeDtypeStruct((tile_rows // 2, tile_cols // 2, 4 * width), BF16),
        in_specs=[pl.BlockSpec(memory_space=pltpu.VMEM)] * 8,
        out_specs=pl.BlockSpec(memory_space=pltpu.VMEM),
        scratch_shapes=[
            pltpu.VMEM((3, 2, width, width // 2), BF16),
            pltpu.VMEM((3, count, width), BF16),
            pltpu.VMEM((3, count, width), BF16),
            pltpu.VMEM((heads, count, count), F32),
            pltpu.VMEM((2, count, width // 4), BF16),
            pltpu.VMEM((2, tile_cols, width // 4), BF16),
            pltpu.VMEM((3, count, heads), F32),
            pltpu.VMEM((8, 128), F32),
            pltpu.VMEM((rows, 8, 128), F32),
            pltpu.VMEM((rows, unit, lanes), BF16),
            pltpu.VMEM((rows, unit, lanes), BF16),
            pltpu.VMEM((rows, unit, lanes), F32),
            pltpu.VMEM((rows, unit, lanes), BF16),
            pltpu.VMEM((rows, unit, lanes), BF16),
            pltpu.VMEM((pairs, count, lanes), F32),
            pltpu.VMEM((2, count, lanes), F32),
            dma((2, 5, rows)),
            dma((2, 2, rows)),
            dma((4,)),
            dma((4,)),
            dma((rows,)),
            dma((rows,)),
            dma((rows,)),
            dma((rows,)),
            dma((rows,)),
            dma((rows,)),
        ],
        compiler_params=pltpu.CompilerParams(
            collective_id=0, has_side_effects=True, vmem_limit_bytes=60 * 1024 * 1024),
    )(
        x.reshape(count, width), ratios, w, retention.reshape(heads, count),
        credit.reshape(1, width), gain.reshape(1, width),
        scale.reshape(1, 4 * width), offset.reshape(1, 4 * width),
    )


def solution(mesh):
    return jax.shard_map(
        body,
        mesh=mesh,
        in_specs=(
            P("row", "col", None),
            P(),
            P(None, "row", None),
            P(None, "row", "col"),
            P(),
            P(),
            P(),
            P(),
        ),
        out_specs=P("row", "col", None),
        check_vma=False,
    )
```

time: 377 us -> 85.3 us (0.23)
  waiting for transfers between devices: 221 us -> 0 us
  Pallas kernels: 0 us -> 81.1 us
  other arithmetic: 45 us -> 0 us
  blocking collectives: 40.7 us -> 0 us
  matrix products: 25.9 us -> 0 us
  local copies, waits for them, and re-layouts: 17.6 us -> 3.39 us
  between operations: 14.1 us -> 0.01 us
  starting transfers between devices: 9.26 us -> 0 us
    all_gather x3 -> x0, waiting for transfers between devices: 221 us -> none  [the longest x2 140 us: entering(): everything = jax.tree.map(lambda part: lax.all_gather(part, axis), array)]
    pallas_call x0 -> x1, Pallas kernels: none -> 81.1 us  [body(): pl.pallas_call(functools.partial(kernel, rows, cols, tile_rows, tile_cols...]
    unnamed x1 -> x0, blocking collectives: 40.7 us -> none
    select_n x32 -> x0, other arithmetic: 37.7 us -> none  [hop(): return jax.tree.map(lambda a, b: jnp.where(reached, a, b), new, before)]
    dot_general x21 -> x0, matrix products: 25.9 us -> none  [the longest x16 15.9 us: head_mix(): return jnp.dot(pair_weight, value_head, preferred_element_type=jnp.float32)]
    ppermute x4 -> x0, starting transfers between devices: 9.18 us -> none  [the longest x2 6.6 us: extended(): lax.ppermute(tail, axis, [(i, (i + 1) % count) for i in range(ends)])]
    reshape x7 -> x1, local copies, waits for them, and re-layouts: 9.22 us -> 1.52 us  [body(): retention.reshape(heads, count)]
    slice x10 -> x0, local copies, waits for them, and re-layouts: 4.64 us -> none  [the longest x1 1.03 us: body(): image_embeddings[:, :-1, :quarter]]
  transfers between devices with their start and end apart: 7 -> 0, of which waited for: 3 -> 0; matrix products, arithmetic and copies ran while one was open for 14% -> 0% of each run, Pallas kernels for 0% -> 0%
where the time goes in v1:
time: 85.3 us; the launch traced here: 84.5 us
  Pallas kernels  81.1 us (95%)
  local copies, waits for them, and re-layouts  3.39 us (4%)
    pallas_call x1, Pallas kernels, body(): pl.pallas_call(functools.partial(kernel, rows, cols, tile_rows, tile_cols...  81.1 us
    unnamed x1, local copies, waits for them, and re-layouts  1.87 us

profile of v1, /device:TPU:0, one launch (start us, length us, event | category | flops | bytes accessed | tf_op | source)
XLA Modules:
  0.0 84.5 jit_solution(6696453444611577661)
XLA Ops:
  0.0 1.5 %reshape.19.ret_ref = f32[16,256]{1,0:T(8,128)} reshape(f32[16,8,32]{2,1,0:T(8,128)} %param.11) | data formatting | bytes 32768 | tf_op jit(solution)/shard_map/reshape | solution.py:531
  1.5 81.1 %shard_map.82 = bf16[4,16,4096]{2,1,0:T(8,128)(2,1)} custom-call(bf16[256,1024]{1,0:T(8,128)(2,1)} %bitcast.5, f32[3,1024]{1,0:T(4,128)} %ratio_ref.1, bf16[3,64,1024]{2,1,0:T(8,128)(2,1)} %w_ref.1, f32[16,256]{1,0:T(8,128)} %reshape.19.ret_ref, f32[1,1024]{1,0:T(1,128)} %bitcast.8, f32[1,1024]{1,0:T(1,128)} %bitcast.9, f32[1,4096]{1,0:T(1,128)} %bitcast.6, ...), custom_call_target="tpu_custom_call" | custom-call | tf_op jit(solution)/shard_map/pallas_call | solution.py:495
  82.6 1.9 %copy.10 = bf16[4,16,4096]{2,1,0:T(8,128)(2,1)} copy(bf16[4,16,4096]{2,1,0:T(8,128)(2,1)} %shard_map.82) | data formatting | bytes 1048576

commit v2 on v1

--- a/solution.py
+++ b/solution.py
@@ -22,7 +22,7 @@
     rows, cols, tile_rows, tile_cols, heads,
     x_ref, ratio_ref, w_ref, ret_ref, credit_ref, gain_ref, scale_ref, offset_ref,
     out_ref,
-    wf, mx, proj, decay, halo_side, halo_row, run_c, mine, totals, states, arrived, scan_f, leaving,
+    wf, mx, proj, decay, halo_side, halo_row, run_c, mine, totals, kept_all, states, arrived, scan_f, leaving,
     entering, block, stats,
     w_send, w_recv, halo_send, halo_recv, t_send, t_recv, a_send, a_recv, b_send, b_recv,
 ):
@@ -46,18 +46,32 @@
     q12 = plane - 1 - q
 
     barrier = pltpu.get_barrier_semaphore()
-
-    def greet(o, carry):
-        pl.semaphore_signal(barrier, inc=1, device_id={"row": (row + o) % rows}, device_id_type=MESH)
-        return carry
-
-    lax.fori_loop(1, rows, greet, 0)
     right, left = (col + 1) % cols, (col + cols - 1) % cols
+    down_row, up_row = (row + 1) % rows, (row + rows - 1) % rows
+    can_up, can_down = z < depth - 1, z > 0
+    has_next, has_previous = row < rows - 1, row > 0
+
+    def greet(target):
+        pl.semaphore_signal(barrier, inc=1, device_id=target, device_id_type=MESH)
+
+    greet({"row": z * plane + q1})
+    greet({"row": z * plane + q2})
     for other in (right, left, mate):
-        pl.semaphore_signal(barrier, inc=1, device_id={"col": other}, device_id_type=MESH)
-    pl.semaphore_wait(barrier, rows + 2)
-
-    down_row, up_row = (row + 1) % rows, (row + rows - 1) % rows
+        greet({"col": other})
+    for there, target in (
+        (can_up, (row + plane) % rows), (can_down, (row + rows - plane) % rows),
+        (has_next, down_row), (has_previous, up_row),
+    ):
+        @pl.when(there)
+        def _():
+            greet({"row": target})
+
+    expected = (
+        5 + can_up.astype(jnp.int32) + can_down.astype(jnp.int32)
+        + has_next.astype(jnp.int32) + has_previous.astype(jnp.int32)
+    )
+    pl.semaphore_wait(barrier, expected)
+
     halos = [
         pltpu.make_async_remote_copy(
             x_ref.at[:, 0:quarter], halo_side.at[0], halo_send.at[0], halo_recv.at[0],
@@ -72,11 +86,9 @@
             x_ref.at[0:tile_cols, 3 * quarter:], halo_row.at[1],
             halo_send.at[3], halo_recv.at[3], device_id={"row": up_row}, device_id_type=MESH),
     ]
-    for h in halos:
-        h.start()
 
     def sl(g):
-        return pl.ds(1, 2) if g == 0 else pl.ds(0, 1)
+        return (g + 1) % 3
 
     def place(g, side, src):
         return wf.at[sl(g), side, pl.ds(pl.multiple_of(src * share, share), share), :]
@@ -103,8 +115,6 @@
             ref, ref, w_send.at[g, MATE, src], w_recv.at[g, side, src],
             device_id=targets[MATE], device_id_type=MESH).wait_recv()
 
-    can_up, can_down = z < depth - 1, z > 0
-
     def own_step(g):
         @pl.when(can_up)
         def _():
@@ -170,6 +180,19 @@
         lax.fori_loop(1, rows, one, 0)
 
     own_step(0)
+    own_step(1)
+    halos[0].start()
+    halos[1].start()
+
+    @pl.when(has_next)
+    def _():
+        halos[2].start()
+
+    @pl.when(has_previous)
+    def _():
+        halos[3].start()
+
+    own_step(2)
 
     at = pl.ds(pl.multiple_of(row * share, share), share)
     for p in range(3):
@@ -208,14 +231,39 @@
         total_copy(o).start()
         return carry
 
-    lax.fori_loop(1, rows, total_send, 0)
-
-    z_step(0, 1) if depth > 1 else None
-    first_step(0, 0)
-    second_step(0, 0)
-
-    for h in halos:
-        h.wait()
+    def z_steps(groups, d):
+        if d < depth:
+            for g in groups:
+                z_step(g, d)
+
+    def first_steps(groups, d):
+        if d < depth:
+            for g in groups:
+                first_step(g, d)
+
+    def second_steps(groups, d):
+        if d < depth:
+            for g in groups:
+                second_step(g, d)
+
+    early = (0, 1)
+    z_steps(early, 1)
+    first_steps(early, 0)
+    second_steps(early, 0)
+
+    halos[0].wait()
+    halos[1].wait()
+
+    @pl.when(has_next)
+    def _():
+        halos[2].wait_send()
+        halos[3].wait_recv()
+
+    @pl.when(has_previous)
+    def _():
+        halos[3].wait_send()
+        halos[2].wait_recv()
+
     token = iota((count, quarter), 0)
     place_in_row = token % tile_cols
     x0 = x_ref[:, 0:quarter].astype(F32)
@@ -238,15 +286,6 @@
             c = ratio_ref[p:p + 1, span]
             mx[p, :, span] = (xs * c + shifted[part] * (1.0 - c)).astype(BF16)
 
-    for d in range(2, depth):
-        z_step(0, d)
-        first_step(0, d - 1)
-        second_step(0, d - 1)
-    if depth > 1:
-        first_step(0, depth - 1)
-        second_step(0, depth - 1)
-    own_step(1)
-
     earlier = iota((count, count), 0) > iota((count, count), 1)
     diagonal = iota((count, count), 0) == iota((count, count), 1)
 
@@ -257,9 +296,17 @@
         decay[h] = jnp.where(diagonal, 0.0, jnp.exp(exponent))
         return carry
 
-    lax.fori_loop(0, heads, decays, 0)
-
-    mate_wait(0)
+    for d in range(2, depth):
+        z_steps(early, d)
+        first_steps(early, d - 1)
+        second_steps(early, d - 1)
+        if d == 2:
+            lax.fori_loop(0, heads // 2, decays, 0)
+    z_steps((2,), 1)
+    first_steps(early, depth - 1)
+    first_steps((2,), 0)
+    lax.fori_loop(heads // 2 if depth > 2 else 0, heads, decays, 0)
+    second_steps(early, depth - 1)
 
     def project(p):
         for side in range(2):
@@ -272,8 +319,15 @@
 
             lax.fori_loop(0, half_w // 256, chunk, 0)
 
+    mate_wait(0)
     project(1)
+    z_steps((2,), 2)
+    first_steps((2,), 1)
+    mate_wait(1)
     project(2)
+    for d in range(3, depth):
+        z_steps((2,), d)
+        first_steps((2,), d - 1)
 
     lane = iota((count, lanes), 1)
     low = lane < hd
@@ -311,16 +365,14 @@
         a_copy(o).start()
         return carry
 
+    lax.fori_loop(1, rows, total_send, 0)
     lax.fori_loop(1, rows, a_start, 0)
     arrived[row] = states[row]
 
-    z_step(1, 1) if depth > 1 else None
-    first_step(1, 0)
-    second_step(1, 0)
-    if depth > 2:
-        z_step(1, 2)
-        first_step(1, 1)
-        second_step(1, 1)
+    if depth > 1:
+        first_steps((2,), depth - 1)
+    for d in range(depth - 1):
+        second_steps((2,), d)
 
     def from_all(dst, send_sem, recv_sem):
         def one(o, carry):
@@ -336,8 +388,13 @@
     from_all(arrived, a_send, a_recv)
     head = (row * unit) // hd
 
+    everyone = totals[...]
+    here = iota(everyone.shape, 2) == head
+    kept_all[...] = jnp.broadcast_to(
+        jnp.exp(jnp.sum(jnp.where(here, everyone, 0.0), axis=2, keepdims=True)), everyone.shape)
+
     def kept(j):
-        return jnp.exp(picked(totals[j], head))[0:1, :]
+        return kept_all[j][0:1, :]
 
     def forward(j, acc):
         scan_f[j] = acc
@@ -364,14 +421,9 @@
     lax.fori_loop(1, rows, b_start, 0)
     entering[row] = leaving[row]
 
-    for d in range(3, depth):
-        z_step(1, d)
-        first_step(1, d - 1)
-        second_step(1, d - 1)
     if depth > 1:
-        first_step(1, depth - 1)
-        second_step(1, depth - 1)
-    mate_wait(1)
+        second_steps((2,), depth - 1)
+    mate_wait(2)
     project(0)
 
     def halves(value):
@@ -456,7 +508,7 @@
         return carry
 
     lax.fori_loop(1, rows, drain, 0)
-    for g in range(2):
+    for g in range(3):
         def z_drain(zz, carry):
             src = zz * plane + q
 
@@ -507,6 +559,7 @@
             pltpu.VMEM((3, count, heads), F32),
             pltpu.VMEM((8, 128), F32),
             pltpu.VMEM((rows, 8, 128), F32),
+            pltpu.VMEM((rows, 8, 128), F32),
             pltpu.VMEM((rows, unit, lanes), BF16),
             pltpu.VMEM((rows, unit, lanes), BF16),
             pltpu.VMEM((rows, unit, lanes), F32),
@@ -514,8 +567,8 @@
             pltpu.VMEM((rows, unit, lanes), BF16),
             pltpu.VMEM((pairs, count, lanes), F32),
             pltpu.VMEM((2, count, lanes), F32),
-            dma((2, 5, rows)),
-            dma((2, 2, rows)),
+            dma((3, 5, rows)),
+            dma((3, 2, rows)),
             dma((4,)),
             dma((4,)),
             dma((rows,)),

time: 85.3 us -> 73.3 us (0.86)
  Pallas kernels: 81.1 us -> 69.6 us
    pallas_call x1, Pallas kernels: 81.1 us -> 69.6 us  [body(): pl.pallas_call(functools.partial(kernel, rows, cols, tile_rows, tile_cols...]
where the time goes in v2:
time: 73.3 us; the launch traced here: 73 us
  Pallas kernels  69.6 us (95%)
  local copies, waits for them, and re-layouts  3.39 us (5%)
    pallas_call x1, Pallas kernels, body(): pl.pallas_call(functools.partial(kernel, rows, cols, tile_rows, tile_cols...  69.6 us
    unnamed x1, local copies, waits for them, and re-layouts  1.87 us
    reshape x1, local copies, waits for them, and re-layouts, body(): retention.reshape(heads, count)  1.52 us

profile of v2, /device:TPU:0, one launch (start us, length us, event | category | flops | bytes accessed | tf_op | source)
XLA Modules:
  0.0 73.0 jit_solution(17501217470570766019)
XLA Ops:
  0.0 1.5 %reshape.19.ret_ref = f32[16,256]{1,0:T(8,128)} reshape(f32[16,8,32]{2,1,0:T(8,128)} %param.11) | data formatting | bytes 32768 | tf_op jit(solution)/shard_map/reshape | solution.py:584
  1.5 69.6 %shard_map.82 = bf16[4,16,4096]{2,1,0:T(8,128)(2,1)} custom-call(bf16[256,1024]{1,0:T(8,128)(2,1)} %bitcast.5, f32[3,1024]{1,0:T(4,128)} %ratio_ref.1, bf16[3,64,1024]{2,1,0:T(8,128)(2,1)} %w_ref.1, f32[16,256]{1,0:T(8,128)} %reshape.19.ret_ref, f32[1,1024]{1,0:T(1,128)} %bitcast.8, f32[1,1024]{1,0:T(1,128)} %bitcast.9, f32[1,4096]{1,0:T(1,128)} %bitcast.6, ...), custom_call_target="tpu_custom_call" | custom-call | tf_op jit(solution)/shard_map/pallas_call | solution.py:547
  71.2 1.9 %copy.10 = bf16[4,16,4096]{2,1,0:T(8,128)(2,1)} copy(bf16[4,16,4096]{2,1,0:T(8,128)(2,1)} %shard_map.82) | data formatting | bytes 1048576

commit v3 on v2

--- a/solution.py
+++ b/solution.py
@@ -199,7 +199,7 @@
         for side in range(2):
             wf[p, side, at, :] = w_ref[p, :, side * half_w:(side + 1) * half_w]
 
-    ret = ret_ref[...]
+    ret = jnp.concatenate([ret_ref[:, r, :] for r in range(tile_rows)], axis=1)
     tri = (iota((count, count), 0) >= iota((count, count), 1)).astype(F32)
     running_c = lax.dot_general(tri, ret, (((1,), (1,)), ((), ())), precision=HIGH, preferred_element_type=F32)
     running_r = lax.dot_general(ret, tri, (((1,), (1,)), ((), ())), precision=HIGH, preferred_element_type=F32)
@@ -231,25 +231,30 @@
         total_copy(o).start()
         return carry
 
+    issued = set()
+
+    def once(step, g, d):
+        if d < depth and (step, g, d) not in issued:
+            issued.add((step, g, d))
+            step(g, d)
+
     def z_steps(groups, d):
-        if d < depth:
-            for g in groups:
-                z_step(g, d)
+        for g in groups:
+            once(z_step, g, d)
 
     def first_steps(groups, d):
-        if d < depth:
-            for g in groups:
-                first_step(g, d)
+        for g in groups:
+            once(first_step, g, d)
 
     def second_steps(groups, d):
-        if d < depth:
-            for g in groups:
-                second_step(g, d)
+        for g in groups:
+            once(second_step, g, d)
 
     early = (0, 1)
     z_steps(early, 1)
     first_steps(early, 0)
-    second_steps(early, 0)
+    z_steps(early, 2)
+    first_steps(early, 1)
 
     halos[0].wait()
     halos[1].wait()
@@ -296,16 +301,22 @@
         decay[h] = jnp.where(diagonal, 0.0, jnp.exp(exponent))
         return carry
 
-    for d in range(2, depth):
+    for d in range(3, depth):
         z_steps(early, d)
         first_steps(early, d - 1)
-        second_steps(early, d - 1)
-        if d == 2:
-            lax.fori_loop(0, heads // 2, decays, 0)
     z_steps((2,), 1)
+    first_steps((2,), 0)
     first_steps(early, depth - 1)
-    first_steps((2,), 0)
-    lax.fori_loop(heads // 2 if depth > 2 else 0, heads, decays, 0)
+    lax.fori_loop(0, heads // 2, decays, 0)
+    z_steps((2,), 2)
+    first_steps((2,), 1)
+    for d in range(depth - 1):
+        second_steps(early, d)
+    lax.fori_loop(heads // 2, heads, decays, 0)
+    for d in range(3, depth):
+        z_steps((2,), d)
+        first_steps((2,), d - 1)
+    first_steps((2,), depth - 1)
     second_steps(early, depth - 1)
 
     def project(p):
@@ -321,13 +332,8 @@
 
     mate_wait(0)
     project(1)
-    z_steps((2,), 2)
-    first_steps((2,), 1)
     mate_wait(1)
     project(2)
-    for d in range(3, depth):
-        z_steps((2,), d)
-        first_steps((2,), d - 1)
 
     lane = iota((count, lanes), 1)
     low = lane < hd
@@ -369,8 +375,6 @@
     lax.fori_loop(1, rows, a_start, 0)
     arrived[row] = states[row]
 
-    if depth > 1:
-        first_steps((2,), depth - 1)
     for d in range(depth - 1):
         second_steps((2,), d)
 
@@ -421,8 +425,7 @@
     lax.fori_loop(1, rows, b_start, 0)
     entering[row] = leaving[row]
 
-    if depth > 1:
-        second_steps((2,), depth - 1)
+    second_steps((2,), depth - 1)
     mate_wait(2)
     project(0)
 
@@ -581,7 +584,7 @@
         compiler_params=pltpu.CompilerParams(
             collective_id=0, has_side_effects=True, vmem_limit_bytes=60 * 1024 * 1024),
     )(
-        x.reshape(count, width), ratios, w, retention.reshape(heads, count),
+        x.reshape(count, width), ratios, w, retention,
         credit.reshape(1, width), gain.reshape(1, width),
         scale.reshape(1, 4 * width), offset.reshape(1, 4 * width),
     )

time: 73.3 us -> 67.1 us (0.915)
  Pallas kernels: 69.6 us -> 65 us
  local copies, waits for them, and re-layouts: 3.39 us -> 1.87 us
    pallas_call x1, Pallas kernels: 69.6 us -> 65 us  [body(): pl.pallas_call(functools.partial(kernel, rows, cols, tile_rows, tile_cols...]
    reshape x1 -> x0, local copies, waits for them, and re-layouts: 1.52 us -> none  [body(): retention.reshape(heads, count)]
where the time goes in v3:
time: 67.1 us; the launch traced here: 66.9 us
  Pallas kernels  65 us (97%)
  local copies, waits for them, and re-layouts  1.87 us (3%)
    pallas_call x1, Pallas kernels, body(): pl.pallas_call(functools.partial(kernel, rows, cols, tile_rows, tile_cols...  65 us
    unnamed x1, local copies, waits for them, and re-layouts  1.87 us

profile of v3, /device:TPU:0, one launch (start us, length us, event | category | flops | bytes accessed | tf_op | source)
XLA Modules:
  0.0 66.9 jit_solution(10516044917617979797)
XLA Ops:
  0.0 65.0 %shard_map.82 = bf16[4,16,4096]{2,1,0:T(8,128)(2,1)} custom-call(bf16[256,1024]{1,0:T(8,128)(2,1)} %bitcast.5, f32[3,1024]{1,0:T(4,128)} %ratio_ref.1, bf16[3,64,1024]{2,1,0:T(8,128)(2,1)} %w_ref.1, f32[16,8,32]{2,1,0:T(8,128)} %ret_ref.1, f32[1,1024]{1,0:T(1,128)} %bitcast.8, f32[1,1024]{1,0:T(1,128)} %bitcast.9, f32[1,4096]{1,0:T(1,128)} %bitcast.6, ...), custom_call_target="tpu_custom_call" | custom-call | tf_op jit(solution)/shard_map/pallas_call | solution.py:550
  65.0 1.9 %copy.10 = bf16[4,16,4096]{2,1,0:T(8,128)(2,1)} copy(bf16[4,16,4096]{2,1,0:T(8,128)(2,1)} %shard_map.82) | data formatting | bytes 1048576
